TPU v7x, 256 devices: a whole 4x4x8 slice. The times are simulated.
256 devices in a mesh: tile: 16 (over z, core), bank: 16 (over y, x).
Axes of the slice: x: 4, y: 4, z: 8, core: 2. Of those that a mesh axis runs over, the one named last changes fastest.
Arguments:
- volume: bfloat16 [1024, 1024, 128], P('tile', 'bank'), may hold values from -6 to 6
- pick_list: int32 [3, 16, 16, 16], P(None, 'tile', 'bank'), may hold values from 0 to 1023, as said below
- box_counts: int32 [16, 16], P('tile', 'bank'), may hold values from 1 to 16, as said below
- orientations: int32 [16, 16, 16, 128], P('tile', 'bank'), may hold values from 0 to 255, all different within a row
- orient_weight: int32 [16, 16, 16, 128], P('tile', 'bank'), may hold values from 1 to 4
- reference_bank: bfloat16 [256, 20, 4096], P('bank'), may hold values from -6 to 6
Outputs:
- class_sums: float32 [256, 20, 4096], P('bank')
- weight_sums: float32 [256, 20], P('bank')
Inputs may be any that keep to these rules, and one draw needn't show every extreme that they name: pick_list[0, t, b, s] lies in [t * 64, (t + 1) * 64), pick_list[1, t, b, s] in [b * 64, (b + 1) * 64), and pick_list[2, t, b, s] in [0, 32]. `box_counts`: every device has at least one live slot and some device has all 16. The 128 orientations of a slot are distinct.
All inputs are finite; a program needn't handle non-finite values.
Results may differ from a plain program's by a relative error of at most 0.012.
Values may be sent and summed in bfloat16 or wider, within the bound.
A program may use at most 128 MiB of HBM per device.

v0:
```python
import jax
import jax.numpy as jnp
from jax import lax
from jax.sharding import PartitionSpec as P

B = 96
L = 16
R = 256
F = 4096
EPSILON = 1e-06


def extended(block, sides, width):
    for axis, dim in sides:
        count = lax.axis_size(axis)
        forward = [(i, i + 1) for i in range(count - 1)]
        backward = [(target, source) for source, target in forward]
        low = lax.ppermute(
            lax.slice_in_dim(block, block.shape[dim] - width, None, axis=dim), axis, forward
        )
        high = lax.ppermute(lax.slice_in_dim(block, 0, width, axis=dim), axis, backward)
        block = jnp.concatenate([low, block, high], axis=dim)
    return block


def fourier_table():
    samples = jnp.arange(B).astype(jnp.float32)
    terms = jnp.arange(L)
    frequency = jnp.where(terms <= L // 2, terms, terms - L // 2).astype(jnp.float32)
    angles = 2.0 * jnp.pi * frequency[:, None] * samples[None, :] / B
    table = jnp.where((terms <= L // 2)[:, None], jnp.cos(angles), jnp.sin(angles)) / jnp.sqrt(
        jnp.float32(B)
    )
    table_half = table.astype(jnp.bfloat16)
    return (table_half, table_half.astype(jnp.float32))


def box_features(box_cube, table_half, table_full):
    first = jnp.dot(
        box_cube.reshape(B * B, B), table_half.T, preferred_element_type=jnp.float32
    ).reshape(B, B, L)
    second = jnp.einsum("xyc,by->xbc", first, table_full, precision=lax.Precision.HIGHEST)
    third = jnp.einsum("xbc,ax->abc", second, table_full, precision=lax.Precision.HIGHEST)
    return third.reshape(L * L * L).astype(jnp.bfloat16)


def norms_of(features):
    feature_wide = features.astype(jnp.float32)
    return jnp.sqrt(jnp.mean(feature_wide * feature_wide, axis=1) + EPSILON)


def correlate(features, box_norm, bank_rows):
    scores = jnp.einsum("if,rcf->irc", features, bank_rows, preferred_element_type=jnp.float32)
    bank_wide = bank_rows.astype(jnp.float32)
    ref_norm = jnp.sqrt(jnp.mean(bank_wide * bank_wide, axis=2) + EPSILON)
    return scores / (F * box_norm[:, None, None] * ref_norm[None])


def accumulate(multiplicity, correl, features):
    weights = (multiplicity.astype(jnp.float32)[:, :, None] * jnp.maximum(correl, 0.0)).astype(
        jnp.bfloat16
    )
    class_sums = jnp.einsum("irc,if->rcf", weights, features, preferred_element_type=jnp.float32)
    weight_sums = jnp.sum(weights.astype(jnp.float32), axis=0)
    return (class_sums, weight_sums)


def score_local(box_rows, box_multiplicity, reference_bank):
    local_rows = reference_bank.shape[0]
    row_start = lax.axis_index("bank") * local_rows
    local_multiplicity = lax.dynamic_slice_in_dim(box_multiplicity, row_start, local_rows, 1)
    box_norm = norms_of(box_rows)
    correl = correlate(box_rows, box_norm, reference_bank)
    return accumulate(local_multiplicity, correl, box_rows)


def body(volume, pick_list, box_counts, orientations, orient_weight, reference_bank):
    table_half, table_full = fourier_table()
    half_box = B // 2
    padded = extended(volume, (("tile", 0), ("bank", 1)), half_box)
    offset_x = lax.axis_index("tile") * volume.shape[0]
    offset_y = lax.axis_index("bank") * volume.shape[1]
    coords = jnp.stack(
        [pick_list[0, 0, 0] - offset_x, pick_list[1, 0, 0] - offset_y, pick_list[2, 0, 0]], axis=1
    )

    def extract_one(corner):
        box_cube = lax.dynamic_slice(padded, (corner[0], corner[1], corner[2]), (B, B, B))
        return box_features(box_cube, table_half, table_full)

    features = lax.map(extract_one, coords)
    slots = pick_list.shape[3]
    live_slots = jnp.arange(slots) < box_counts[0, 0]
    matches = orientations[0, 0][:, :, None] == jnp.arange(R)[None, None, :]
    multiplicity = jnp.sum(
        jnp.where(matches, orient_weight[0, 0][:, :, None].astype(jnp.float32), 0.0), axis=1
    )
    multiplicity = jnp.where(live_slots[:, None], multiplicity, 0.0).astype(jnp.bfloat16)
    group_features, group_multiplicity = (
        lax.all_gather(features, "bank", axis=0, tiled=True),
        lax.all_gather(multiplicity, "bank", axis=0, tiled=True),
    )
    class_sums, weight_sums = score_local(group_features, group_multiplicity, reference_bank)
    class_sums, weight_sums = lax.psum((class_sums, weight_sums), "tile")
    return (class_sums, weight_sums)


def solution(mesh):
    in_specs = (
        P("tile", "bank", None),
        P(None, "tile", "bank", None),
        P("tile", "bank"),
        P("tile", "bank", None, None),
        P("tile", "bank", None, None),
        P("bank", None, None),
    )
    out_specs = (P("bank", None, None), P("bank", None))
    return jax.shard_map(body, mesh=mesh, in_specs=in_specs, out_specs=out_specs, check_vma=False)
```

profile of v0, /device:TPU:2, one launch (start us, length us, event | category | flops | bytes accessed | tf_op | source)
XLA Modules:
  0.0 504.5 jit_solution(12485962151624641500)
XLA Ops:
  12.7 3.8 collective-permute-done.1
  19.2 3.4 collective-permute-start.2
  22.6 3.7 collective-permute-start.3
  26.4 31.6 %collective-permute-done.2 = bf16[160,48,128]{2,1,0:T(8,128)(2,1)} collective-permute-done((bf16[160,48,128]{2,1,0:T(8,128)(2,1)}, bf16[160,48,128]{2,1,0:T(8,128)(2,1)}, u32[]{:S(2)}, u32[]{:S(2)}) %collective-permute-start.2) | collective-permute-done | bytes 1966112 | tf_op jit(solution)/shard_map/ppermute | solution.py:18
  58.0 3.7 collective-permute-done.3
  61.7 5.3 %pad_maximum_fusion = bf16[160,160,128]{2,1,0:T(8,128)(2,1)} fusion(bf16[160,48,128]{2,1,0:T(8,128)(2,1)} %collective-permute-done.3, bf16[160,64,128]{2,1,0:T(8,128)(2,1)S(1)} %constant_dynamic-update-slice_fusion, bf16[160,48,128]{2,1,0:T(8,128)(2,1)} %collective-permute-done.2), kind=kLoop, calls=%fused_computation.29 | loop fusion | flops 19660800 | bytes 13107200 | tf_op jit(solution)/shard_map/concatenate | solution.py:22
  67.0 213.7 %while.13 = (s32[]{:T(128)}, bf16[16,4096]{1,0:T(8,128)(2,1)}, s32[16,3]{0,1:T(4,128)S(1)}, bf16[160,160,128]{2,1,0:T(8,128)(2,1)}, f32[96]{0:T(128)S(1)}, /*ind...) while((s32[]{:T(128)}, bf16[16,4096]{1,0:T(8,128)(2,1)}, ...), condition=%wide.region_2.3_spmd.clone.clone.clone, body=%wide.region_1.2_spmd.clone.clone.clone.sunk | while | flops 61371912 | bytes 3794567 | solution.py:91
  73.4 3.4 fusion.77
  86.7 3.4 fusion.77
  100.0 3.4 fusion.77
  113.4 3.4 fusion.77
  126.7 3.4 fusion.77
  140.1 3.4 fusion.77
  153.4 3.4 fusion.77
  233.5 3.4 fusion.77
  246.8 3.4 fusion.77
  260.2 3.4 fusion.77
  282.3 24.8 %all_gather.6 = bf16[256,256]{1,0:T(8,128)(2,1)S(1)} all-gather(bf16[16,256]{1,0:T(8,128)(2,1)S(1)} %select_convert_fusion), channel_id=1, replica_groups=mesh['tile'=16,'bank'=16] {'bank'}, dimensions={0}, use_global_device_ids=true | all-gather | bytes 139264 | tf_op jit(solution)/shard_map/all_gather | solution.py:101
  308.0 43.4 %all-gather.2.cloned.1.call-done = bf16[256,4096]{1,0:T(8,128)(2,1)} async-done(((bf16[16,4096]{1,0:T(8,128)(2,1)}), bf16[256,4096]{1,0:T(8,128)(2,1)}) %all-gather.2.cloned.1.call-update) | async-done | bytes 2097168 | tf_op jit(solution)/shard_map/all_gather | solution.py:100
  353.4 4.0 convert_reduce_fusion
  357.5 3.7 fusion.32
  361.1 26.1 %psum.15 = f32[16,20]{1,0:T(8,128)} all-reduce(f32[16,20]{1,0:T(8,128)S(1)} %get-tuple-element.140), channel_id=1, replica_groups=mesh['tile'=16,'bank'=16] {'tile'}, use_global_device_ids=true, to_apply=%region_7.8 | all-reduce | flops 320 | bytes 2560 | tf_op jit(solution)/shard_map/psum | solution.py:104
  387.3 102.2 %all-reduce.2.cloned.1.call-done = f32[16,20,4096]{2,1,0:T(8,128)} async-done(((f32[16,20,4096]{2,1,0:T(8,128)}), f32[16,20,4096]{2,1,0:T(8,128)}) %all-reduce.2.cloned.1.call-update) | async-done | bytes 5242896 | tf_op jit(solution)/shard_map/psum | solution.py:104
  489.5 8.2 %copy.33 = f32[16,20,4096]{2,0,1:T(8,128)} copy(f32[16,20,4096]{2,1,0:T(8,128)} %all-reduce.2.cloned.1.call-done) | data formatting | bytes 10485760
  (160 shorter events, 103.1 us)
Async XLA Ops:
  7.2 344.2 %all-gather.2.cloned.1.call-start = ((), (), s32[]{:S(2)}) async-start(), calls=%async_computation | async-start | bytes 2228224 | tf_op jit(solution)/shard_map/all_gather | solution.py:100
  7.2 5.3 %copy-start.1 = (bf16[64,64,128]{2,1,0:T(8,128)(2,1)S(1)}, bf16[64,64,128]{2,1,0:T(8,128)(2,1)}, u32[]{:S(2)}) copy-start(bf16[64,64,128]{2,1,0:T(8,128)(2,1)} %param.8) | copy-start | bytes 3145732
  8.8 3.6 collective-permute-start
  10.6 5.8 %collective-permute-start.1 = (bf16[48,64,128]{2,1,0:T(8,128)(2,1)S(1)}, bf16[48,64,128]{2,1,0:T(8,128)(2,1)S(1)}, u32[]{:S(2)}, u32[]{:S(2)}) collective-permute-start(bf16[48,64,128]{2,1,0:T(8,128)(2,1)S(1)} %get-tuple-element.135), channel_id=1, source_target_pairs={{16,0},{32,16},{48,32},{64,48},{80,64},{96,80},{112,96},{128,112},... | collective-permute-start | bytes 2359304 | tf_op jit(solution)/shard_map/ppermute | solution.py:21
  16.5 9.8 %copy-start.5 = (s32[3,1,1,16]{3,2,1,0:T(1,128)S(1)}, s32[3,1,1,16]{3,2,1,0:T(1,128)}, u32[]{:S(2)}) copy-start(s32[3,1,1,16]{3,2,1,0:T(1,128)} %param.9) | copy-start | bytes 580
  19.2 38.8 %collective-permute-start.2 = (bf16[160,48,128]{2,1,0:T(8,128)(2,1)}, bf16[160,48,128]{2,1,0:T(8,128)(2,1)}, u32[]{:S(2)}, u32[]{:S(2)}) collective-permute-start(bf16[160,48,128]{2,1,0:T(8,128)(2,1)} %get-tuple-element.133), channel_id=1, source_target_pairs={{0,1},{1,2},{2,3},{3,4},{4,5},{5,6},{6,7},{7,8},{8,9},{9,10},{10,1... | collective-permute-start | bytes 5898248 | tf_op jit(solution)/shard_map/ppermute | solution.py:18
  22.6 39.1 %collective-permute-start.3 = (bf16[160,48,128]{2,1,0:T(8,128)(2,1)}, bf16[160,48,128]{2,1,0:T(8,128)(2,1)}, u32[]{:S(2)}, u32[]{:S(2)}) collective-permute-start(bf16[160,48,128]{2,1,0:T(8,128)(2,1)} %get-tuple-element.134), channel_id=1, source_target_pairs={{1,0},{2,1},{3,2},{4,3},{5,4},{6,5},{7,6},{8,7},{9,8},{10,9},{11,1... | collective-permute-start | bytes 5898248 | tf_op jit(solution)/shard_map/ppermute | solution.py:21
  67.0 214.4 %copy-start.4 = (s32[1,1,16,128]{3,2,1,0:T(8,128)S(1)}, s32[1,1,16,128]{3,2,1,0:T(8,128)}, u32[]{:S(2)}) copy-start(s32[1,1,16,128]{3,2,1,0:T(8,128)} %param.12) | copy-start | bytes 24580
  67.0 214.5 %copy-start.3 = (s32[1,1,16,128]{3,2,1,0:T(8,128)S(1)}, s32[1,1,16,128]{3,2,1,0:T(8,128)}, u32[]{:S(2)}) copy-start(s32[1,1,16,128]{3,2,1,0:T(8,128)} %param.11) | copy-start | bytes 24580
  67.0 240.2 %copy-start.2 = (bf16[16,20,4096]{2,0,1:T(8,128)(2,1)S(1)}, bf16[16,20,4096]{2,0,1:T(8,128)(2,1)}, u32[]{:S(2)}) copy-start(bf16[16,20,4096]{2,0,1:T(8,128)(2,1)} %param.13) | copy-start | bytes 7864324
  280.7 208.7 %all-reduce.2.cloned.1.call-start = ((), (), s32[]{:S(2)}) async-start(), calls=%async_computation.1 | async-start | bytes 12582912 | tf_op jit(solution)/shard_map/psum | solution.py:104
  353.4 4.0 copy-start
Sparse Core Ops, SparseCore 0:
  280.9 70.4 all-gather.1
  361.3 128.1 all-reduce.1
where the time goes:
time: 507 us; the launch traced here: 505 us
  waiting for transfers between devices  185 us (36%)
  matrix products  94.5 us (19%)
  loops' own time  88.9 us (18%)
  local copies, waits for them, and re-layouts  50.9 us (10%)
  blocking collectives  50.9 us (10%)
  between operations  14.9 us (3%)
  starting transfers between devices  10.3 us (2%)
  other arithmetic  8.83 us (2%)
    psum x1, waiting for transfers between devices, body(): class_sums, weight_sums = lax.psum((class_sums, weight_sums), 'tile')  102 us
    another operation x1, loops' own time, body(): features = lax.map(extract_one, coords)  88.9 us
    dot_general x16, matrix products, box_features(): jnp.dot(box_cube.reshape(B * B, B), table_half.T, preferred_element_type=...  53.8 us
    all_gather x1, waiting for transfers between devices, body(): lax.all_gather(features, 'bank', axis=0, tiled=True)  43.4 us
    ppermute x2, waiting for transfers between devices, extended(): lax.ppermute(lax.slice_in_dim(block, block.shape[dim] - width, None, axis...  32.1 us
    dot_general x16, matrix products, box_features(): jnp.einsum('xyc,by->xbc', first, table_full, precision=lax.Precision.HIGH...  27.1 us
    psum x1, blocking collectives, body(): class_sums, weight_sums = lax.psum((class_sums, weight_sums), 'tile')  26.1 us
    all_gather x1, blocking collectives, body(): lax.all_gather(multiplicity, 'bank', axis=0, tiled=True)  24.8 us
  transfers between devices with their start and end apart: 6, of which 6 were waited for; matrix products, arithmetic and copies ran while one was open for 0% of the time, Pallas kernels for 0%

commit v1 on v0

--- a/solution.py
+++ b/solution.py
@@ -96,8 +96,11 @@
         jnp.where(matches, orient_weight[0, 0][:, :, None].astype(jnp.float32), 0.0), axis=1
     )
     multiplicity = jnp.where(live_slots[:, None], multiplicity, 0.0).astype(jnp.bfloat16)
+    manage_the_side = lambda u, axis_name: jnp.concatenate(
+        jax.lax.all_to_all(jnp.stack([u] * jax.lax.axis_size(axis_name)), axis_name, 0, 0), axis=0
+    )
     group_features, group_multiplicity = (
-        lax.all_gather(features, "bank", axis=0, tiled=True),
+        manage_the_side(features, "bank"),
         lax.all_gather(multiplicity, "bank", axis=0, tiled=True),
     )
     class_sums, weight_sums = score_local(group_features, group_multiplicity, reference_bank)

time: 507 us -> 492 us (0.970)
  waiting for transfers between devices: 185 us -> 145 us
  blocking collectives: 50.9 us -> 84.6 us
  local copies, waits for them, and re-layouts: 50.9 us -> 31.9 us
  starting transfers between devices: 10.3 us -> 19.8 us
    all_gather x1 -> x0, waiting for transfers between devices: 43.4 us -> none  [body(): lax.all_gather(features, 'bank', axis=0, tiled=True)]
    dynamic_update_slice x16, local copies, waits for them, and re-layouts: 24.3 us -> 3.65 us  [body(): features = lax.map(extract_one, coords)]
    psum x1, blocking collectives: 26.1 us -> 45.5 us  [body(): class_sums, weight_sums = lax.psum((class_sums, weight_sums), 'tile')]
    all_gather x1, blocking collectives: 24.8 us -> 39.1 us  [body(): lax.all_gather(multiplicity, 'bank', axis=0, tiled=True)]
    all_to_all x0 -> x1, starting transfers between devices: none -> 9.56 us  [body(): jax.lax.all_to_all(jnp.stack([u] * jax.lax.axis_size(axis_name)), axis_na...]
  transfers between devices with their start and end apart: 6 -> 6, of which waited for: 6 -> 5; matrix products, arithmetic and copies ran while one was open for 0% -> 1% of each run, Pallas kernels for 0% -> 0%
where the time goes in v1:
time: 492 us; the launch traced here: 489 us
  waiting for transfers between devices  145 us (29%)
  matrix products  94.6 us (19%)
  loops' own time  89.9 us (18%)
  blocking collectives  84.6 us (17%)
  local copies, waits for them, and re-layouts  31.9 us (6%)
  starting transfers between devices  19.8 us (4%)
  between operations  14.9 us (3%)
  other arithmetic  8.99 us (2%)
    psum x1, waiting for transfers between devices, body(): class_sums, weight_sums = lax.psum((class_sums, weight_sums), 'tile')  105 us
    another operation x1, loops' own time, body(): features = lax.map(extract_one, coords)  89.9 us
    dot_general x16, matrix products, box_features(): jnp.dot(box_cube.reshape(B * B, B), table_half.T, preferred_element_type=...  53.9 us
    psum x1, blocking collectives, body(): class_sums, weight_sums = lax.psum((class_sums, weight_sums), 'tile')  45.5 us
    all_gather x1, blocking collectives, body(): lax.all_gather(multiplicity, 'bank', axis=0, tiled=True)  39.1 us
    ppermute x2, waiting for transfers between devices, extended(): lax.ppermute(lax.slice_in_dim(block, block.shape[dim] - width, None, axis...  32.1 us
    dot_general x16, matrix products, box_features(): jnp.einsum('xyc,by->xbc', first, table_full, precision=lax.Precision.HIGH...  27.1 us
  transfers between devices with their start and end apart: 6, of which 5 were waited for; matrix products, arithmetic and copies ran while one was open for 1% of the time, Pallas kernels for 0%

profile of v1, /device:TPU:2, one launch (start us, length us, event | category | flops | bytes accessed | tf_op | source)
XLA Modules:
  0.0 489.4 jit_solution(227973970344860183)
XLA Ops:
  12.6 3.8 collective-permute-done.1
  19.1 3.4 collective-permute-start.2
  22.5 3.8 collective-permute-start.3
  26.4 31.6 %collective-permute-done.2 = bf16[160,48,128]{2,1,0:T(8,128)(2,1)} collective-permute-done((bf16[160,48,128]{2,1,0:T(8,128)(2,1)}, bf16[160,48,128]{2,1,0:T(8,128)(2,1)}, u32[]{:S(2)}, u32[]{:S(2)}) %collective-permute-start.2) | collective-permute-done | bytes 1966112 | tf_op jit(solution)/shard_map/ppermute | solution.py:18
  58.0 3.7 collective-permute-done.3
  61.6 5.3 %pad_maximum_fusion = bf16[160,160,128]{2,1,0:T(8,128)(2,1)} fusion(bf16[160,48,128]{2,1,0:T(8,128)(2,1)} %collective-permute-done.3, bf16[160,64,128]{2,1,0:T(8,128)(2,1)S(1)} %constant_dynamic-update-slice_fusion, bf16[160,48,128]{2,1,0:T(8,128)(2,1)} %collective-permute-done.2), kind=kLoop, calls=%fused_computation.29 | loop fusion | flops 19660800 | bytes 13107200 | tf_op jit(solution)/shard_map/concatenate | solution.py:22
  67.0 194.1 %while.13 = (s32[]{:T(128)}, bf16[16,4096]{1,0:T(8,128)(2,1)S(1)}, s32[16,3]{0,1:T(4,128)S(1)}, bf16[160,160,128]{2,1,0:T(8,128)(2,1)}, f32[96]{0:T(128)S(1)}, /...) while((s32[]{:T(128)}, bf16[16,4096]{1,0:T(8,128)(2,1)S(1)}, ...), condition=%wide.region_2.3_spmd.clone.clone.clone, body=%wide.region_1.2_spmd.clone.clone.clone.sunk | while | flops 61371912 | bytes 3794567 | solution.py:91
  73.2 3.4 fusion.69
  85.3 3.4 fusion.69
  97.4 3.4 fusion.69
  109.6 3.4 fusion.69
  121.7 3.4 fusion.69
  133.8 3.4 fusion.69
  146.0 3.4 fusion.69
  158.1 3.4 fusion.69
  170.2 3.4 fusion.69
  243.0 3.4 fusion.69
  262.7 9.6 %all-to-all-start = ((bf16[16,16,4096]{2,1,0:T(8,128)(2,1)}), bf16[16,16,4096]{2,1,0:T(8,128)(2,1)S(1)}, u32[]{:S(2)}, u32[]{:S(2)}) async-start(bf16[16,16,4096]{2,1,0:T(8,128)(2,1)} %stack.5), calls=%async_computation | async-start | bytes 4194304 | tf_op jit(solution)/shard_map/all_to_all | solution.py:100
  273.7 39.1 %all_gather.3 = bf16[256,256]{1,0:T(8,128)(2,1)S(1)} all-gather(bf16[16,256]{1,0:T(8,128)(2,1)S(1)} %select_convert_fusion), channel_id=1, replica_groups=mesh['tile'=16,'bank'=16] {'bank'}, dimensions={0}, use_global_device_ids=true | all-gather | bytes 139264 | tf_op jit(solution)/shard_map/all_gather | solution.py:104
  316.1 4.0 convert_reduce_fusion
  320.1 3.7 fusion.49
  323.8 45.5 %psum.15 = f32[16,20]{1,0:T(8,128)} all-reduce(f32[16,20]{1,0:T(8,128)S(1)} %get-tuple-element.140), channel_id=1, replica_groups=mesh['tile'=16,'bank'=16] {'tile'}, use_global_device_ids=true, to_apply=%region_7.8 | all-reduce | flops 320 | bytes 2560 | tf_op jit(solution)/shard_map/psum | solution.py:107
  369.3 105.0 %all-reduce.2.cloned.1.call-done = f32[16,20,4096]{2,1,0:T(8,128)} async-done(((f32[16,20,4096]{2,1,0:T(8,128)}), f32[16,20,4096]{2,1,0:T(8,128)}) %all-reduce.2.cloned.1.call-update) | async-done | bytes 5242896 | tf_op jit(solution)/shard_map/psum | solution.py:107
  474.3 8.2 %copy.33 = f32[16,20,4096]{2,0,1:T(8,128)} copy(f32[16,20,4096]{2,1,0:T(8,128)} %all-reduce.2.cloned.1.call-done) | data formatting | bytes 10485760
  (157 shorter events, 84.3 us)
Async XLA Ops:
  7.2 5.3 %copy-start = (bf16[64,64,128]{2,1,0:T(8,128)(2,1)S(1)}, bf16[64,64,128]{2,1,0:T(8,128)(2,1)}, u32[]{:S(2)}) copy-start(bf16[64,64,128]{2,1,0:T(8,128)(2,1)} %param.8) | copy-start | bytes 3145732
  8.8 3.6 collective-permute-start
  10.6 5.8 %collective-permute-start.1 = (bf16[48,64,128]{2,1,0:T(8,128)(2,1)S(1)}, bf16[48,64,128]{2,1,0:T(8,128)(2,1)S(1)}, u32[]{:S(2)}, u32[]{:S(2)}) collective-permute-start(bf16[48,64,128]{2,1,0:T(8,128)(2,1)S(1)} %get-tuple-element.135), channel_id=1, source_target_pairs={{16,0},{32,16},{48,32},{64,48},{80,64},{96,80},{112,96},{128,112},... | collective-permute-start | bytes 2359304 | tf_op jit(solution)/shard_map/ppermute | solution.py:21
  16.5 9.8 %copy-start.3 = (s32[3,1,1,16]{3,2,1,0:T(1,128)S(1)}, s32[3,1,1,16]{3,2,1,0:T(1,128)}, u32[]{:S(2)}) copy-start(s32[3,1,1,16]{3,2,1,0:T(1,128)} %param.9) | copy-start | bytes 580
  19.1 38.8 %collective-permute-start.2 = (bf16[160,48,128]{2,1,0:T(8,128)(2,1)}, bf16[160,48,128]{2,1,0:T(8,128)(2,1)}, u32[]{:S(2)}, u32[]{:S(2)}) collective-permute-start(bf16[160,48,128]{2,1,0:T(8,128)(2,1)} %get-tuple-element.133), channel_id=1, source_target_pairs={{0,1},{1,2},{2,3},{3,4},{4,5},{5,6},{6,7},{7,8},{8,9},{9,10},{10,1... | collective-permute-start | bytes 5898248 | tf_op jit(solution)/shard_map/ppermute | solution.py:18
  22.5 39.1 %collective-permute-start.3 = (bf16[160,48,128]{2,1,0:T(8,128)(2,1)}, bf16[160,48,128]{2,1,0:T(8,128)(2,1)}, u32[]{:S(2)}, u32[]{:S(2)}) collective-permute-start(bf16[160,48,128]{2,1,0:T(8,128)(2,1)} %get-tuple-element.134), channel_id=1, source_target_pairs={{1,0},{2,1},{3,2},{4,3},{5,4},{6,5},{7,6},{8,7},{9,8},{10,9},{11,1... | collective-permute-start | bytes 5898248 | tf_op jit(solution)/shard_map/ppermute | solution.py:21
  262.7 10.3 %copy-start.2 = (s32[1,1,16,128]{3,2,1,0:T(8,128)S(1)}, s32[1,1,16,128]{3,2,1,0:T(8,128)}, u32[]{:S(2)}) copy-start(s32[1,1,16,128]{3,2,1,0:T(8,128)} %param.12) | copy-start | bytes 24580
  262.7 10.3 %copy-start.1 = (s32[1,1,16,128]{3,2,1,0:T(8,128)S(1)}, s32[1,1,16,128]{3,2,1,0:T(8,128)}, u32[]{:S(2)}) copy-start(s32[1,1,16,128]{3,2,1,0:T(8,128)} %param.11) | copy-start | bytes 24580
  262.7 52.8 %all-to-all-start = ((bf16[16,16,4096]{2,1,0:T(8,128)(2,1)}), bf16[16,16,4096]{2,1,0:T(8,128)(2,1)S(1)}, u32[]{:S(2)}, u32[]{:S(2)}) async-start(bf16[16,16,4096]{2,1,0:T(8,128)(2,1)} %stack.5), calls=%async_computation | async-start | bytes 4194304 | tf_op jit(solution)/shard_map/all_to_all | solution.py:100
  272.2 202.1 %all-reduce.2.cloned.1.call-start = ((), (), s32[]{:S(2)}) async-start(), calls=%async_computation.1 | async-start | bytes 12582912 | tf_op jit(solution)/shard_map/psum | solution.py:107
Sparse Core Ops, SparseCore 0:
  323.9 150.3 all-reduce.1
